TPU v7x, 32 devices: a whole 2x2x4 slice. The times are simulated.
32 devices in a mesh: rows: 8 (over z, y), grp: 4 (over x, core).
Axes of the slice: x: 2, y: 2, z: 4, core: 2. Of those that a mesh axis runs over, the one named last changes fastest.
Arguments:
- features: bfloat16 [4096, 512], P(('rows', 'grp')), may hold values from -6 to 6
- tile_entries: bfloat16 [64, 64, 1024], P(('rows', 'grp'))
- tile_columns: int32 [64, 16], P(('rows', 'grp')), may hold values from 0 to 63, as said below
- tiles_per_row: int32 [64], P(('rows', 'grp')), may hold values from 1 to 16, as said below
- rev_vals: bfloat16 [64, 64, 1024], P(('rows', 'grp'))
- rev_cols: int32 [64, 16], P(('rows', 'grp')), may hold values from 0 to 63, as said below
- rev_count: int32 [64], P(('rows', 'grp')), may hold values from 1 to 16, as said below
- w_first: bfloat16 [512, 512], replicated, may hold values from -0.25 to 0.25
- w_second: bfloat16 [512, 512], replicated, may hold values from -0.25 to 0.25
- cotangent: bfloat16 [4096, 512], P(('rows', 'grp')), may hold values from -0.09375 to 0.09375
Outputs:
- z_out: bfloat16 [4096, 512], P(('rows', 'grp'))
- grad_first: float32 [512, 512], replicated
- grad_second: float32 [512, 512], replicated
Inputs may be any that keep to these rules, and one draw needn't show every extreme that they name: `tile_columns`: within each block row the 16 slots name distinct block columns; for each slot s, the block columns named in slot s over all block rows are all different. `tiles_per_row`: some block row has exactly 16 tiles. `rev_cols`: within each block column the slots name distinct block rows; the live transposed slots of block column c hold exactly the transposes of the live tiles of A in block column c. `rev_count`: some block column has exactly 16 tiles.
All inputs are finite; a program needn't handle non-finite values.
Results may differ from a plain program's by a relative error of at most 0.0062.
Values may be sent and summed in bfloat16 or wider, within the bound.
No kernel may reach another device: no remote copies, remote signals or barrier semaphores. Data moves between devices by JAX's collectives and lax.ppermute only.
A program may use at most 128 MiB of HBM per device.

v0:
```python
import jax
import jax.numpy as jnp
from jax import lax
from jax.sharding import PartitionSpec as P


def active_mask(columns, counts):
    return lax.broadcasted_iota(jnp.int32, columns.shape, 1) < counts[:, None]


def aggregate(panel_vals, strip_columns, strip_count, everyone, own_rows):
    blocks, size_block, span_width = panel_vals.shape
    slot_count = span_width // size_block
    channels = everyone.shape[1]
    block_table = everyone.reshape(-1, size_block, channels)
    weights = active_mask(strip_columns, strip_count).astype(everyone.dtype)
    picked = (block_table[strip_columns] * weights[:, :, None, None]).reshape(
        blocks, slot_count * size_block, channels
    )
    summed_rows = jnp.einsum("bik,bkc->bic", panel_vals, picked, preferred_element_type=jnp.float32)
    return summed_rows.reshape(blocks * size_block, channels) + own_rows.astype(jnp.float32)


def spread_terms(panel_vals, strip_columns, strip_count, grad_rows):
    blocks, size_block, span_width = panel_vals.shape
    slot_count = span_width // size_block
    channels = grad_rows.shape[1]
    products = jnp.einsum(
        "bik,bic->bkc",
        panel_vals,
        grad_rows.reshape(blocks, size_block, channels),
        preferred_element_type=jnp.float32,
    )
    products = products.reshape(blocks * slot_count, size_block, channels)
    targets = strip_columns.reshape(-1)
    slot_active = active_mask(strip_columns, strip_count).reshape(-1)

    def term_rows(first_row, row_count):
        segment_ids = row_count // size_block
        slot_offset = targets - first_row // size_block
        inside_bound = slot_active & (slot_offset >= 0) & (slot_offset < segment_ids)
        labels = jnp.where(inside_bound, slot_offset, segment_ids)
        summed_rows = jax.ops.segment_sum(products, labels, num_segments=segment_ids + 1)
        return summed_rows[:segment_ids].reshape(row_count, channels)

    return term_rows


def silu_slope(values):
    sigmoid_part = jax.nn.sigmoid(values)
    return sigmoid_part * (1.0 + values * (1.0 - sigmoid_part))


def to_columns(row_block):
    return lax.all_to_all(row_block, "grp", split_axis=1, concat_axis=0, tiled=True)


def mix_columns(column_block, panel_vals, strip_columns, strip_count):
    everyone = lax.all_gather(column_block, "rows", axis=0, tiled=True)
    return aggregate(panel_vals, strip_columns, strip_count, everyone, column_block)


def shards(
    features,
    tile_entries,
    tile_columns,
    tiles_per_row,
    rev_vals,
    rev_cols,
    rev_count,
    w_first,
    w_second,
    cotangent,
):
    panel_vals, strip_columns, strip_count = (
        lax.all_gather(tile_entries, "grp", axis=0, tiled=True),
        lax.all_gather(tile_columns, "grp", axis=0, tiled=True),
        lax.all_gather(tiles_per_row, "grp", axis=0, tiled=True),
    )

    def propagate(row_block):
        column_block = to_columns(row_block)
        summed_rows = mix_columns(column_block, panel_vals, strip_columns, strip_count).astype(
            jnp.bfloat16
        )
        return lax.all_to_all(summed_rows, "grp", split_axis=0, concat_axis=1, tiled=True)

    mixed_first = propagate(features)
    pre_first = jnp.dot(mixed_first, w_first, preferred_element_type=jnp.float32)
    hidden = jax.nn.silu(pre_first).astype(jnp.bfloat16)
    mixed_second = propagate(hidden)
    z_out = jnp.dot(mixed_second, w_second, preferred_element_type=jnp.float32).astype(jnp.bfloat16)
    local_second = jnp.einsum(
        "nh,nk->hk", mixed_second, cotangent, preferred_element_type=jnp.float32
    )
    grad_second = lax.psum(local_second, ("rows", "grp"))
    back_second = jnp.dot(cotangent, w_second.T, preferred_element_type=jnp.float32).astype(
        jnp.bfloat16
    )
    column_block = to_columns(back_second)
    term_rows = spread_terms(panel_vals, strip_columns, strip_count, column_block)
    summed_rows = lax.psum_scatter(
        term_rows(jnp.int32(0), column_block.shape[0] * lax.axis_size("rows")),
        "rows",
        scatter_dimension=0,
        tiled=True,
    )
    summed_rows = summed_rows + column_block.astype(jnp.float32)
    back_hidden = lax.all_to_all(summed_rows, "grp", split_axis=0, concat_axis=1, tiled=True)
    back_first = (back_hidden * silu_slope(pre_first)).astype(jnp.bfloat16)
    local_first = jnp.einsum(
        "nh,nk->hk", mixed_first, back_first, preferred_element_type=jnp.float32
    )
    grad_first = lax.psum(local_first, ("rows", "grp"))
    return (z_out, grad_first, grad_second)


def solution(mesh):
    placed = (
        P(("rows", "grp"), None),
        P(("rows", "grp"), None, None),
        P(("rows", "grp"), None),
        P(("rows", "grp")),
        P(("rows", "grp"), None, None),
        P(("rows", "grp"), None),
        P(("rows", "grp")),
        P(),
        P(),
        P(("rows", "grp"), None),
    )
    return jax.shard_map(
        shards,
        mesh=mesh,
        in_specs=placed,
        out_specs=(P(("rows", "grp"), None), P(), P()),
        check_vma=False,
    )
```

profile of v0, /device:TPU:0, one launch (start us, length us, event | category | flops | bytes accessed | tf_op | source)
XLA Modules:
  0.0 358.8 jit_solution(1867615093499603882)
XLA Ops:
  7.2 1.1 copy.33
  8.3 8.6 %all_to_all.105 = bf16[128,4,128]{0,2,1:T(8,128)(2,1)S(1)} all-to-all(bf16[128,4,128]{0,2,1:T(8,128)(2,1)S(1)} %bitcast.96), channel_id=1, replica_groups=mesh['rows'=8,'grp'=4] {'grp'}, dimensions={1} | all-to-all | bytes 262144 | tf_op jit(solution)/shard_map/all_to_all | solution.py:55
  18.5 1.2 dynamic-slice
  21.3 4.3 %all-reduce = s32[8]{0:T(128)S(1)} all-reduce(s32[8]{0:T(128)S(1)} %dynamic-update-slice), channel_id=1, replica_groups=mesh['rows'=8,'grp'=4] {'grp'}, use_global_device_ids=true, to_apply=%add | all-reduce | flops 8 | bytes 64
  25.6 5.3 %all-gather = s32[4,2,16]{2,1,0:T(2,128)S(1)} all-gather(s32[1,2,16]{2,1,0:T(2,128)} %bitcast.98), channel_id=1, replica_groups=mesh['rows'=8,'grp'=4] {'grp'}, dimensions={0}, use_global_device_ids=true | all-gather | bytes 640 | tf_op jit(solution)/shard_map/all_gather | solution.py:77
  31.2 27.2 %all-gather.5.cloned.1.call-done = bf16[4096,128]{1,0:T(8,128)(2,1)} async-done(((bf16[512,128]{1,0:T(8,128)(2,1)}), bf16[4096,128]{1,0:T(8,128)(2,1)}) %all-gather.5.cloned.1.call-update) | async-done | bytes 1048592 | tf_op jit(solution)/shard_map/all_gather | solution.py:59
  58.4 2.2 gather_fusion
  60.6 2.2 bitcast_multiply_fusion.1
  62.8 12.7 %all-gather.7.cloned.1.call-done = bf16[8,64,1024]{2,1,0:T(8,128)(2,1)} async-done(((bf16[2,64,1024]{2,1,0:T(8,128)(2,1)}), bf16[8,64,1024]{2,1,0:T(8,128)(2,1)}) %all-gather.7.cloned.1.call-update) | async-done | bytes 1048592 | tf_op jit(solution)/shard_map/all_gather | solution.py:76
  75.5 2.4 fusion.11
  78.1 7.2 %all_to_all.106 = bf16[4,128,128]{1,2,0:T(8,128)(2,1)S(1)} all-to-all(bf16[4,128,128]{1,2,0:T(8,128)(2,1)S(1)} %add_convert_fusion.1), channel_id=1, replica_groups=mesh['rows'=8,'grp'=4] {'grp'}, dimensions={0} | all-to-all | bytes 262144 | tf_op jit(solution)/shard_map/all_to_all | solution.py:86
  85.6 7.7 %all_to_all.107 = bf16[128,4,128]{2,0,1:T(8,128)(2,1)} all-to-all(bf16[128,4,128]{2,0,1:T(8,128)(2,1)S(1)} %copy_bitcast_fusion.1), channel_id=1, replica_groups=mesh['rows'=8,'grp'=4] {'grp'}, dimensions={1} | all-to-all | bytes 262144 | tf_op jit(solution)/shard_map/all_to_all | solution.py:55
  94.3 3.3 all-to-all-start.4
  97.9 4.4 %all-to-all-done.4 = bf16[128,4,128]{2,0,1:T(8,128)(2,1)S(1)} async-done(((bf16[128,4,128]{2,0,1:T(8,128)(2,1)}), bf16[128,4,128]{2,0,1:T(8,128)(2,1)S(1)}, u32[]{:S(2)}, u32[]{:S(2)}) %all-to-all-start.4) | async-done | bytes 131104 | tf_op jit(solution)/shard_map/all_to_all | solution.py:55
  102.3 2.7 convolution_bitcast_fusion
  105.0 5.4 %copy.39 = f32[8,1024,128]{2,1,0:T(8,128)} copy(f32[8,1024,128]{1,2,0:T(8,128)} %convolution_bitcast_fusion) | data formatting | bytes 8388608 | tf_op jit(solution)/shard_map/bik,bic->bkc/dot_general | solution.py:28
  110.6 13.6 %scatter_fusion = f32[65,64,128]{2,1,0:T(8,128)S(1)} fusion(f32[65,64,128]{2,1,0:T(8,128)S(1)} %broadcast_in_dim.6, s32[128]{0:T(128)S(1)} %fusion.6, f32[128,64,128]{2,1,0:T(8,128)} %bitcast.79), kind=kCustom, calls=%fused_computation.2 | custom fusion | flops 1048576 | bytes 12583424 | tf_op jit(solution)/shard_map/scatter-add | solution.py:43
  124.2 1.5 slice.8
  125.7 7.9 %all-gather.9.cloned.1.call-done = bf16[4096,128]{1,0:T(8,128)(2,1)} async-done(((bf16[512,128]{1,0:T(8,128)(2,1)}), bf16[4096,128]{1,0:T(8,128)(2,1)}) %all-gather.9.cloned.1.call-update) | async-done | bytes 1048592 | tf_op jit(solution)/shard_map/all_gather | solution.py:59
  133.6 2.2 gather_fusion.1
  135.8 1.6 bitcast_multiply_fusion
  138.4 7.2 %all_to_all.108 = bf16[4,128,128]{2,1,0:T(8,128)(2,1)S(1)} all-to-all(bf16[4,128,128]{2,1,0:T(8,128)(2,1)S(1)} %add_convert_fusion), channel_id=1, replica_groups=mesh['rows'=8,'grp'=4] {'grp'}, dimensions={0} | all-to-all | bytes 262144 | tf_op jit(solution)/shard_map/all_to_all | solution.py:86
  145.7 58.0 %reduce-scatter.2.cloned.1.call-done = f32[512,128]{1,0:T(8,128)} async-done(((f32[4096,128]{1,0:T(8,128)}), f32[512,128]{1,0:T(8,128)}) %reduce-scatter.2.cloned.1.call-update) | async-done | bytes 262160 | tf_op jit(solution)/shard_map/reduce_scatter | solution.py:102
  203.7 1.7 convert_add_fusion
  205.4 3.4 all-to-all-start.5
  208.8 1.3 fusion.10
  210.1 4.7 %all-to-all-done.5 = f32[4,128,128]{2,1,0:T(8,128)S(1)} async-done(((f32[4,128,128]{2,1,0:T(8,128)}), f32[4,128,128]{2,1,0:T(8,128)S(1)}, u32[]{:S(2)}, u32[]{:S(2)}) %all-to-all-start.5) | async-done | bytes 262176 | tf_op jit(solution)/shard_map/all_to_all | solution.py:109
  214.8 1.3 fusion.2
  216.1 0.9 convolution_convert_fusion.1
  217.0 131.9 %all-reduce.4.cloned.1.call-done = (f32[512,512]{1,0:T(8,128)}, f32[512,512]{1,0:T(8,128)}) async-done(((f32[512,512]{1,0:T(8,128)}, f32[512,512]{1,0:T(8,128)}), (f32[512,512]{1,0:T(8,128)}, f32[512,512]{1,0:T(8,128)})) %all-reduce.4.cloned.1.call-update) | async-done | bytes 2097168 | tf_op jit(solution)/shard_map/psum | solution.py:114
  348.9 2.4 copy.53
  351.3 1.0 copy.54
  (46 shorter events, 5.9 us)
Async XLA Ops:
  7.2 86.1 %copy-start = (bf16[512,512]{1,0:T(8,128)(2,1)S(1)}, bf16[512,512]{1,0:T(8,128)(2,1)}, u32[]{:S(2)}) copy-start(bf16[512,512]{1,0:T(8,128)(2,1)} %param.15) | copy-start | bytes 1572868
  7.2 51.3 %all-gather.5.cloned.1.call-start = ((), (), s32[]{:S(2)}) async-start(), calls=%async_computation.7 | async-start | bytes 1179648 | tf_op jit(solution)/shard_map/all_gather | solution.py:59
  17.7 57.8 %all-gather.7.cloned.1.call-start = ((), (), s32[]{:S(2)}) async-start(), calls=%async_computation.8 | async-start | bytes 1310720 | tf_op jit(solution)/shard_map/all_gather | solution.py:76
  18.5 115.1 %all-gather.9.cloned.1.call-start = ((), (), s32[]{:S(2)}) async-start(), calls=%async_computation.9 | async-start | bytes 1179648 | tf_op jit(solution)/shard_map/all_gather | solution.py:59
  62.8 22.4 %copy-start.5 = (bf16[512,512]{1,0:T(8,128)(2,1)S(1)}, bf16[512,512]{1,0:T(8,128)(2,1)}, u32[]{:S(2)}) copy-start(bf16[512,512]{1,0:T(8,128)(2,1)} %param.14) | copy-start | bytes 1572868
  77.9 15.4 %copy-start.6 = (bf16[128,512]{1,0:T(8,128)(2,1)S(1)}, bf16[128,512]{1,0:T(8,128)(2,1)}, u32[]{:S(2)}) copy-start(bf16[128,512]{1,0:T(8,128)(2,1)} %param.16) | copy-start | bytes 393220
  77.9 24.3 %copy-start.1 = (bf16[8,64,1024]{2,1,0:T(8,128)(2,1)S(1)}, bf16[8,64,1024]{2,1,0:T(8,128)(2,1)}, u32[]{:S(2)}) copy-start(bf16[8,64,1024]{2,1,0:T(8,128)(2,1)} %all-gather.7.cloned.1.call-done) | copy-start | bytes 3145732
  94.3 7.9 %all-to-all-start.4 = ((bf16[128,4,128]{2,0,1:T(8,128)(2,1)}), bf16[128,4,128]{2,0,1:T(8,128)(2,1)S(1)}, u32[]{:S(2)}, u32[]{:S(2)}) async-start(bf16[128,4,128]{2,0,1:T(8,128)(2,1)} %bitcast.76), calls=%async_computation.4 | async-start | bytes 262144 | tf_op jit(solution)/shard_map/all_to_all | solution.py:55
  97.7 106.0 %reduce-scatter.2.cloned.1.call-start = ((), (), s32[]{:S(2)}) async-start(), calls=%async_computation.10 | async-start | bytes 2359296 | tf_op jit(solution)/shard_map/reduce_scatter | solution.py:102
  135.8 1.6 copy-start.2
  137.4 0.9 copy-start.3
  205.4 9.4 %all-to-all-start.5 = ((f32[4,128,128]{2,1,0:T(8,128)}), f32[4,128,128]{2,1,0:T(8,128)S(1)}, u32[]{:S(2)}, u32[]{:S(2)}) async-start(f32[4,128,128]{2,1,0:T(8,128)} %bitcast.28), calls=%async_computation.6 | async-start | bytes 524288 | tf_op jit(solution)/shard_map/all_to_all | solution.py:109
  208.8 140.1 %all-reduce.4.cloned.1.call-start = ((), (), s32[]{:S(2)}) async-start(), calls=%async_computation.11 | async-start | bytes 4194304 | tf_op jit(solution)/shard_map/psum | solution.py:114
  348.9 2.4 copy-start.4
Sparse Core Ops, SparseCore 0:
  17.9 40.5 all-gather.4
  60.0 15.4 all-gather.6
  93.4 40.1 all-gather.8
  137.0 66.6 reduce-scatter.1
  216.3 132.6 all-reduce.3
where the time goes:
time: 360 us; the launch traced here: 359 us
  waiting for transfers between devices  247 us (69%)
  blocking collectives  40.2 us (11%)
  local copies, waits for them, and re-layouts  20.5 us (6%)
  other arithmetic  19.3 us (5%)
  between operations  14.7 us (4%)
  matrix products  9.67 us (3%)
  starting transfers between devices  6.93 us (2%)
    psum x1, waiting for transfers between devices, shards(): grad_first = lax.psum(local_first, ('rows', 'grp'))  132 us
    reduce_scatter x1, waiting for transfers between devices, shards(): lax.psum_scatter(term_rows(jnp.int32(0), column_block.shape[0] * lax.axis...  58 us
    all_gather x2, waiting for transfers between devices, mix_columns(): everyone = lax.all_gather(column_block, 'rows', axis=0, tiled=True)  35.2 us
    all_to_all x2, blocking collectives, to_columns(): lax.all_to_all(row_block, 'grp', split_axis=1, concat_axis=0, tiled=True)  16.3 us
    all_to_all x2, blocking collectives, propagate(): lax.all_to_all(summed_rows, 'grp', split_axis=0, concat_axis=1, tiled=True)  14.3 us
    scatter-add x1, other arithmetic, term_rows(): jax.ops.segment_sum(products, labels, num_segments=segment_ids + 1)  13.6 us
    all_gather x1, waiting for transfers between devices, shards(): lax.all_gather(tile_entries, 'grp', axis=0, tiled=True)  12.7 us
  transfers between devices with their start and end apart: 7, of which 7 were waited for; matrix products, arithmetic and copies ran while one was open for 11% of the time, Pallas kernels for 0%

commit v1 on v0

--- a/solution.py
+++ b/solution.py
@@ -2,6 +2,12 @@
 import jax.numpy as jnp
 from jax import lax
 from jax.sharding import PartitionSpec as P
+from jax.lax import all_gather
+
+
+def match_columns(named_axis, inp):
+    y2 = all_gather(inp, named_axis)
+    return jnp.sum(y2, axis=0)
 
 
 def active_mask(columns, counts):
@@ -111,7 +117,7 @@
     local_first = jnp.einsum(
         "nh,nk->hk", mixed_first, back_first, preferred_element_type=jnp.float32
     )
-    grad_first = lax.psum(local_first, ("rows", "grp"))
+    grad_first = match_columns(("rows", "grp"), local_first)
     return (z_out, grad_first, grad_second)
 
 

time: 360 us -> 523 us (1.45)
  waiting for transfers between devices: 247 us -> 390 us
  other arithmetic: 19.3 us -> 33.2 us
  blocking collectives: 40.2 us -> 50.2 us
    all_gather x0 -> x1, waiting for transfers between devices: none -> 180 us  [match_columns(): y2 = all_gather(inp, named_axis)]
    reduce_sum x0 -> x1, other arithmetic: none -> 13.3 us  [match_columns(): return jnp.sum(y2, axis=0)]
    all_gather x1, waiting for transfers between devices: 12.7 us -> 0.02 us  [shards(): lax.all_gather(tile_entries, 'grp', axis=0, tiled=True)]
    psum x1, waiting for transfers between devices: 132 us -> 120 us  [shards(): grad_second = lax.psum(local_second, ('rows', 'grp'))]
    reduce_scatter x1, waiting for transfers between devices: 58 us -> 48 us  [shards(): lax.psum_scatter(term_rows(jnp.int32(0), column_block.shape[0] * lax.axis...]
    all_to_all x0 -> x1, blocking collectives: none -> 8.58 us  [shards(): lax.all_to_all(summed_rows, 'grp', split_axis=0, concat_axis=1, tiled=True)]
    all_gather x2, waiting for transfers between devices: 35.2 us -> 41.3 us  [mix_columns(): everyone = lax.all_gather(column_block, 'rows', axis=0, tiled=True)]
  transfers between devices with their start and end apart: 7 -> 7, of which waited for: 7 -> 5; matrix products, arithmetic and copies ran while one was open for 11% -> 12% of each run, Pallas kernels for 0% -> 0%
where the time goes in v1:
time: 523 us; the launch traced here: 522 us
  waiting for transfers between devices  390 us (75%)
  blocking collectives  50.2 us (10%)
  other arithmetic  33.2 us (6%)
  local copies, waits for them, and re-layouts  20.5 us (4%)
  between operations  15 us (3%)
  matrix products  9.93 us (2%)
    all_gather x1, waiting for transfers between devices, match_columns(): y2 = all_gather(inp, named_axis)  180 us
    psum x1, waiting for transfers between devices, shards(): grad_second = lax.psum(local_second, ('rows', 'grp'))  120 us
    reduce_scatter x1, waiting for transfers between devices, shards(): lax.psum_scatter(term_rows(jnp.int32(0), column_block.shape[0] * lax.axis...  48 us
    all_gather x2, waiting for transfers between devices, mix_columns(): everyone = lax.all_gather(column_block, 'rows', axis=0, tiled=True)  41.3 us
    all_to_all x2, blocking collectives, to_columns(): lax.all_to_all(row_block, 'grp', split_axis=1, concat_axis=0, tiled=True)  16.3 us
    all_to_all x2, blocking collectives, propagate(): lax.all_to_all(summed_rows, 'grp', split_axis=0, concat_axis=1, tiled=True)  14.9 us
    scatter-add x1, other arithmetic, term_rows(): jax.ops.segment_sum(products, labels, num_segments=segment_ids + 1)  13.6 us
    reduce_sum x1, other arithmetic, match_columns(): return jnp.sum(y2, axis=0)  13.3 us
  transfers between devices with their start and end apart: 7, of which 5 were waited for; matrix products, arithmetic and copies ran while one was open for 12% of the time, Pallas kernels for 0%

profile of v1, /device:TPU:0, one launch (start us, length us, event | category | flops | bytes accessed | tf_op | source)
XLA Modules:
  0.0 522.2 jit_solution(15022331372317094167)
XLA Ops:
  7.3 0.7 all-gather.9.cloned.1.call-update
  8.0 1.0 copy.33
  9.0 8.6 %all_to_all.105 = bf16[128,4,128]{0,2,1:T(8,128)(2,1)S(1)} all-to-all(bf16[128,4,128]{0,2,1:T(8,128)(2,1)S(1)} %bitcast.99), channel_id=1, replica_groups=mesh['rows'=8,'grp'=4] {'grp'}, dimensions={1} | all-to-all | bytes 262144 | tf_op jit(solution)/shard_map/all_to_all | solution.py:61
  17.7 0.8 copy.34
  18.5 1.2 fusion
  19.7 0.7 copy.48
  21.9 3.3 all-to-all-start.4
  25.3 5.4 %all-reduce = s32[8]{0:T(128)S(1)} all-reduce(s32[8]{0:T(128)S(1)} %dynamic-update-slice), channel_id=1, replica_groups=mesh['rows'=8,'grp'=4] {'grp'}, use_global_device_ids=true, to_apply=%add | all-reduce | flops 8 | bytes 64
  30.6 5.1 all-gather.1
  36.0 3.9 convolution_bitcast_fusion
  39.9 5.4 %copy.39 = f32[8,1024,128]{2,1,0:T(8,128)} copy(f32[8,1024,128]{1,2,0:T(8,128)} %convolution_bitcast_fusion) | data formatting | bytes 8388608 | tf_op jit(solution)/shard_map/bik,bic->bkc/dot_general | solution.py:34
  45.5 13.6 %scatter_fusion = f32[65,64,128]{2,1,0:T(8,128)S(1)} fusion(f32[65,64,128]{2,1,0:T(8,128)S(1)} %broadcast_in_dim.6, s32[128]{0:T(128)S(1)} %fusion.6, f32[128,64,128]{2,1,0:T(8,128)} %bitcast.81), kind=kCustom, calls=%fused_computation.2 | custom fusion | flops 1048576 | bytes 12583424 | tf_op jit(solution)/shard_map/scatter-add | solution.py:49
  59.1 1.5 slice.8
  61.0 11.0 %all-gather.7.cloned.1.call-done = bf16[4096,128]{1,0:T(8,128)(2,1)} async-done(((bf16[512,128]{1,0:T(8,128)(2,1)}), bf16[4096,128]{1,0:T(8,128)(2,1)}) %all-gather.7.cloned.1.call-update) | async-done | bytes 1048592 | tf_op jit(solution)/shard_map/all_gather | solution.py:65
  71.9 3.4 gather_fusion
  75.3 2.6 bitcast_multiply_fusion.1
  78.6 7.2 %all_to_all.106 = bf16[4,128,128]{1,2,0:T(8,128)(2,1)S(1)} all-to-all(bf16[4,128,128]{1,2,0:T(8,128)(2,1)S(1)} %add_convert_fusion.1), channel_id=1, replica_groups=mesh['rows'=8,'grp'=4] {'grp'}, dimensions={0} | all-to-all | bytes 262144 | tf_op jit(solution)/shard_map/all_to_all | solution.py:92
  86.1 7.7 %all_to_all.107 = bf16[128,4,128]{2,0,1:T(8,128)(2,1)} all-to-all(bf16[128,4,128]{2,0,1:T(8,128)(2,1)S(1)} %copy_bitcast_fusion.1), channel_id=1, replica_groups=mesh['rows'=8,'grp'=4] {'grp'}, dimensions={1} | all-to-all | bytes 262144 | tf_op jit(solution)/shard_map/all_to_all | solution.py:61
  93.9 48.0 %reduce-scatter.2.cloned.1.call-done = f32[512,128]{1,0:T(8,128)} async-done(((f32[4096,128]{1,0:T(8,128)}), f32[512,128]{1,0:T(8,128)}) %reduce-scatter.2.cloned.1.call-update) | async-done | bytes 262160 | tf_op jit(solution)/shard_map/reduce_scatter | solution.py:108
  141.8 1.0 convert_add_fusion
  142.8 8.6 %all_to_all.108 = f32[4,128,128]{2,1,0:T(8,128)S(1)} all-to-all(f32[4,128,128]{2,1,0:T(8,128)S(1)} %bitcast.94), channel_id=1, replica_groups=mesh['rows'=8,'grp'=4] {'grp'}, dimensions={0} | all-to-all | bytes 524288 | tf_op jit(solution)/shard_map/all_to_all | solution.py:115
  151.4 1.3 fusion.2
  152.8 30.3 %all-gather.11.cloned.1.call-done = bf16[4096,128]{1,0:T(8,128)(2,1)} async-done(((bf16[512,128]{1,0:T(8,128)(2,1)}), bf16[4096,128]{1,0:T(8,128)(2,1)}) %all-gather.11.cloned.1.call-update) | async-done | bytes 1048592 | tf_op jit(solution)/shard_map/all_gather | solution.py:65
  183.2 3.4 gather_fusion.1
  186.5 2.5 bitcast_multiply_fusion
  189.9 7.7 %all_to_all.109 = bf16[4,128,128]{2,1,0:T(8,128)(2,1)S(1)} all-to-all(bf16[4,128,128]{2,1,0:T(8,128)(2,1)S(1)} %add_convert_fusion), channel_id=1, replica_groups=mesh['rows'=8,'grp'=4] {'grp'}, dimensions={0} | all-to-all | bytes 262144 | tf_op jit(solution)/shard_map/all_to_all | solution.py:92
  197.8 1.3 fusion.10
  199.1 0.9 convolution_convert_fusion.1
  200.0 180.0 %all-gather.13.cloned.1.call-done = f32[16384,512]{1,0:T(8,128)} async-done(((f32[512,512]{1,0:T(8,128)}), f32[16384,512]{1,0:T(8,128)}) %all-gather.13.cloned.1.call-update) | async-done | bytes 33554448 | tf_op jit(solution)/shard_map/all_gather | solution.py:9
  380.0 13.3 %reduce_sum.9 = f32[512,512]{1,0:T(8,128)} reduce(f32[32,512,512]{2,1,0:T(8,128)} %bitcast.80, f32[]{:T(128)} %constant.26.clone.1), dimensions={0}, to_apply=%region_2.3 | reduce | flops 8126464 | bytes 34603012 | tf_op jit(solution)/shard_map/reduce_sum | solution.py:10
  393.3 119.8 %all-reduce.3.cloned.1.call-done = f32[512,512]{1,0:T(8,128)} async-done(((f32[512,512]{1,0:T(8,128)}), f32[512,512]{1,0:T(8,128)}) %all-reduce.3.cloned.1.call-update) | async-done | bytes 1048592 | tf_op jit(solution)/shard_map/psum | solution.py:102
  513.1 2.3 copy.52
  (50 shorter events, 4.0 us)
Async XLA Ops:
  7.2 11.3 %copy-start = (bf16[512,512]{1,0:T(8,128)(2,1)S(1)}, bf16[512,512]{1,0:T(8,128)(2,1)}, u32[]{:S(2)}) copy-start(bf16[512,512]{1,0:T(8,128)(2,1)} %param.15) | copy-start | bytes 1572868
  7.2 13.2 %copy-start.7 = (u32[32]{0:T(128)S(1)}, u32[32]{0:T(128)}, u32[]{:S(2)}) copy-start(u32[32]{0:T(128)} %constant.32) | copy-start | bytes 388
  7.2 14.4 %copy-start.6 = (s32[2]{0:T(128)S(1)}, s32[2]{0:T(128)}, u32[]{:S(2)}) copy-start(s32[2]{0:T(128)} %param.13) | copy-start | bytes 28
  7.2 23.4 %copy-start.5 = (s32[2,16]{1,0:T(2,128)S(1)}, s32[2,16]{1,0:T(2,128)}, u32[]{:S(2)}) copy-start(s32[2,16]{1,0:T(2,128)} %param.12) | copy-start | bytes 388
  7.2 28.8 %all-gather.9.cloned.1.call-start = ((), (), s32[]{:S(2)}) async-start(), calls=%async_computation.8 | async-start | bytes 1310720 | tf_op jit(solution)/shard_map/all_gather | solution.py:82
  7.9 64.0 %all-gather.7.cloned.1.call-start = ((), (), s32[]{:S(2)}) async-start(), calls=%async_computation.7 | async-start | bytes 1179648 | tf_op jit(solution)/shard_map/all_gather | solution.py:65
  21.9 14.1 %all-to-all-start.4 = ((bf16[128,4,128]{2,0,1:T(8,128)(2,1)}), bf16[128,4,128]{2,0,1:T(8,128)(2,1)S(1)}, u32[]{:S(2)}, u32[]{:S(2)}) async-start(bf16[128,4,128]{2,0,1:T(8,128)(2,1)} %bitcast.77), calls=%async_computation.4 | async-start | bytes 262144 | tf_op jit(solution)/shard_map/all_to_all | solution.py:61
  25.2 116.6 %reduce-scatter.2.cloned.1.call-start = ((), (), s32[]{:S(2)}) async-start(), calls=%async_computation.10 | async-start | bytes 2359296 | tf_op jit(solution)/shard_map/reduce_scatter | solution.py:108
  60.6 122.5 %all-gather.11.cloned.1.call-start = ((), (), s32[]{:S(2)}) async-start(), calls=%async_computation.9 | async-start | bytes 1179648 | tf_op jit(solution)/shard_map/all_gather | solution.py:65
  75.3 2.6 copy-start.1
  77.9 7.9 %copy-start.3 = (bf16[512,512]{1,0:T(8,128)(2,1)S(1)}, bf16[512,512]{1,0:T(8,128)(2,1)}, u32[]{:S(2)}) copy-start(bf16[512,512]{1,0:T(8,128)(2,1)} %param.14) | copy-start | bytes 1572868
  93.8 286.2 %all-gather.13.cloned.1.call-start = ((), (), s32[]{:S(2)}) async-start(), calls=%async_computation.12 | async-start | bytes 34603008 | tf_op jit(solution)/shard_map/all_gather | solution.py:9
  152.8 360.3 %all-reduce.3.cloned.1.call-start = ((), (), s32[]{:S(2)}) async-start(), calls=%async_computation.11 | async-start | bytes 2097152 | tf_op jit(solution)/shard_map/psum | solution.py:102
  189.0 0.9 copy-start.2
  189.0 8.8 %copy-start.4 = (bf16[128,512]{1,0:T(8,128)(2,1)S(1)}, bf16[128,512]{1,0:T(8,128)(2,1)}, u32[]{:S(2)}) copy-start(bf16[128,512]{1,0:T(8,128)(2,1)} %param.16) | copy-start | bytes 393220
Sparse Core Ops, SparseCore 0:
  9.6 19.4 all-gather.8
  31.8 40.1 all-gather.6
  75.5 66.3 reduce-scatter.1
  143.8 39.2 all-gather.10
  186.4 193.5 all-gather.12
  385.1 127.9 all-reduce.2
